TPU v7x, 32 devices: a whole 2x2x4 slice. The times are simulated.
32 devices in a mesh: section: 8 (over z, core), ctx: 4 (over y, x).
Axes of the slice: x: 2, y: 2, z: 4, core: 2. Of those that a mesh axis runs over, the one named last changes fastest.
Arguments:
- gate_q: bfloat16 [8, 512, 4096], P('section', 'ctx'), may hold values from -6 to 6
- gate_k: bfloat16 [8, 512, 4096], P('section', 'ctx'), may hold values from -6 to 6
- value_in: bfloat16 [8, 512, 4096], P('section', 'ctx'), may hold values from -6 to 6
- filter_raw: bfloat16 [8, 512, 4096], P('section', 'ctx'), may hold values from -0.5 to 0.5
- decay_rate: float32 [8, 4096], P('section'), may hold values from 0.25 to 16
- skip_gain: float32 [8, 4096], P('section'), may hold values from -4 to 4
- grad_out: bfloat16 [8, 512, 4096], P('section', 'ctx'), may hold values from -6 to 6
Outputs:
- grad_q: bfloat16 [8, 512, 4096], P('section', 'ctx')
- grad_k: bfloat16 [8, 512, 4096], P('section', 'ctx')
- grad_passed: bfloat16 [8, 512, 4096], P('section', 'ctx')
- filter_grad: bfloat16 [8, 512, 4096], P('section', 'ctx')
- rate_grad: float32 [8, 4096], P('section')
- skip_grad: float32 [8, 4096], P('section')
All inputs are finite; a program needn't handle non-finite values.
Results may differ from a plain program's by a relative error of at most 0.013.
Values may be sent and summed in bfloat16 or wider, within the bound.
A program may use at most 128 MiB of HBM per device.

v0:
```python
import math
import jax
import jax.numpy as jnp
from jax import lax
from jax.sharding import PartitionSpec as P

exact_mode = lax.Precision.HIGHEST


def shifted(x, axis, by):
    size = lax.axis_size(axis)
    pairs = [(i, i + by) for i in range(size) if 0 <= i + by < size]
    return lax.ppermute(x, axis, pairs)


def every_table(parts_count):
    twice = 2 * parts_count
    m_index = jnp.arange(parts_count, dtype=jnp.int32)[:, None, None]
    bin_grid = jnp.arange(twice, dtype=jnp.int32).reshape(parts_count, 2).T[None]
    angle = (m_index * bin_grid % twice).astype(jnp.float32) * (math.pi / parts_count)
    return jnp.stack([jnp.cos(angle), -jnp.sin(angle)], axis=2)


def combined_tables(slot_bins, tok_rows, fft_length):
    factor_len = fft_length // tok_rows
    row_index = jnp.arange(tok_rows, dtype=jnp.int32)
    frequency = slot_bins[:, None] + factor_len * row_index[None, :]
    product = row_index[None, :, None] * frequency[:, None, :] % fft_length
    angle = product.astype(jnp.float32) * (2.0 * math.pi / fft_length)
    cosine = jnp.cos(angle)
    sine = jnp.sin(angle)
    forward_table = jnp.stack(
        [jnp.stack([cosine, -sine], axis=2), jnp.stack([sine, cosine], axis=2)], axis=1
    )
    cos_back = jnp.transpose(cosine, (0, 2, 1))
    sin_back = jnp.transpose(sine, (0, 2, 1))
    inverse_table = jnp.stack(
        [jnp.stack([cos_back, sin_back], axis=2), jnp.stack([-sin_back, cos_back], axis=2)], axis=1
    )
    return (forward_table, inverse_table)


def spectral_middle(stack_mixed, stack_filter, stack_pulled, slot_bins, tok_rows, fft_length):
    forward_table, inverse_table = combined_tables(slot_bins, tok_rows, fft_length)

    def forward(stacked):
        return jnp.einsum(
            "spjc,spjqb->sqbc", stacked.astype(jnp.float32), forward_table, precision=exact_mode
        )

    def inverse(real_part, imag_part):
        stacked = jnp.stack([real_part, imag_part], axis=1)
        return jnp.einsum("sqbc,sqbpj->spjc", stacked, inverse_table, precision=exact_mode).astype(
            jnp.bfloat16
        )

    spec_mix = forward(stack_mixed)
    spec_fil = forward(stack_filter)
    spec_pul = forward(stack_pulled)
    mix_real, mix_imag = (spec_mix[:, 0], spec_mix[:, 1])
    fil_real, fil_imag = (spec_fil[:, 0], spec_fil[:, 1])
    pul_real, pul_imag = (spec_pul[:, 0], spec_pul[:, 1])
    folded_conv = inverse(
        fil_real * mix_real - fil_imag * mix_imag, fil_real * mix_imag + fil_imag * mix_real
    )
    folded_adj = inverse(
        fil_real * pul_real + fil_imag * pul_imag, fil_real * pul_imag - fil_imag * pul_real
    )
    folded_cor = inverse(
        mix_real * pul_real + mix_imag * pul_imag, mix_real * pul_imag - mix_imag * pul_real
    )
    return (folded_conv, folded_adj, folded_cor)


def shards(gate_q, gate_k, value_in, filter_raw, decay_rate, skip_gain, grad_out):
    parts_count = lax.axis_size("ctx")
    my_rank = lax.axis_index("ctx")
    tok_rows = gate_q.shape[1]
    channels = gate_q.shape[2]
    group_rows = tok_rows // parts_count
    seq_length = tok_rows * parts_count
    fft_length = 2 * seq_length
    positions = (my_rank * tok_rows + jnp.arange(tok_rows, dtype=jnp.int32)).astype(
        jnp.float32
    ) / seq_length
    rate_row = decay_rate[0][None, :]
    skip_row = skip_gain[0][None, :]
    envelope = jnp.exp(-rate_row * positions[:, None])
    modulated = filter_raw[0].astype(jnp.float32) * envelope
    filter_bf = modulated.astype(jnp.bfloat16)
    mixed_in = (gate_k[0].astype(jnp.float32) * value_in[0].astype(jnp.float32)).astype(
        jnp.bfloat16
    )
    pulled = (gate_q[0].astype(jnp.float32) * grad_out[0].astype(jnp.float32)).astype(jnp.bfloat16)
    block_shape = (parts_count, group_rows, channels)
    sectioned_mixed, sectioned_filter, sectioned_pulled = (
        lax.all_to_all(
            mixed_in.reshape(block_shape), "ctx", split_axis=0, concat_axis=0, tiled=True
        ),
        lax.all_to_all(
            filter_bf.reshape(block_shape), "ctx", split_axis=0, concat_axis=0, tiled=True
        ),
        lax.all_to_all(pulled.reshape(block_shape), "ctx", split_axis=0, concat_axis=0, tiled=True),
    )
    table_first = every_table(parts_count)

    def first_section(sectioned):
        return jnp.einsum(
            "mgc,mlir->lirgc", sectioned.astype(jnp.float32), table_first, precision=exact_mode
        ).astype(jnp.bfloat16)

    got_mixed, got_filter, got_pulled = (
        lax.all_to_all(
            first_section(sectioned_mixed), "ctx", split_axis=2, concat_axis=2, tiled=True
        ),
        lax.all_to_all(
            first_section(sectioned_filter), "ctx", split_axis=2, concat_axis=2, tiled=True
        ),
        lax.all_to_all(
            first_section(sectioned_pulled), "ctx", split_axis=2, concat_axis=2, tiled=True
        ),
    )

    def unpack(received):
        return received.reshape(2, 2, tok_rows, channels)

    slot_bins = 2 * my_rank + jnp.arange(2, dtype=jnp.int32)
    folded_conv, folded_adj, folded_cor = spectral_middle(
        unpack(got_mixed), unpack(got_filter), unpack(got_pulled), slot_bins, tok_rows, fft_length
    )

    def pack(folded):
        return folded.reshape(2, 2, parts_count, group_rows, channels)

    back_conv, back_adj, back_cor = (
        lax.all_to_all(pack(folded_conv), "ctx", split_axis=2, concat_axis=2, tiled=True),
        lax.all_to_all(pack(folded_adj), "ctx", split_axis=2, concat_axis=2, tiled=True),
        lax.all_to_all(pack(folded_cor), "ctx", split_axis=2, concat_axis=2, tiled=True),
    )
    table_last = table_first / fft_length

    def last_section(received):
        return jnp.einsum(
            "lirgc,mlir->mgc", received.astype(jnp.float32), table_last, precision=exact_mode
        ).astype(jnp.bfloat16)

    home_conv, home_adj, home_cor = (
        lax.all_to_all(last_section(back_conv), "ctx", split_axis=0, concat_axis=0, tiled=True),
        lax.all_to_all(last_section(back_adj), "ctx", split_axis=0, concat_axis=0, tiled=True),
        lax.all_to_all(last_section(back_cor), "ctx", split_axis=0, concat_axis=0, tiled=True),
    )
    conv_out = home_conv.reshape(tok_rows, channels).astype(jnp.float32)
    adjoint = home_adj.reshape(tok_rows, channels).astype(jnp.float32)
    filter_corr = home_cor.reshape(tok_rows, channels).astype(jnp.float32)
    mixed_f = mixed_in.astype(jnp.float32)
    pulled_f = pulled.astype(jnp.float32)
    grad_q_local = (grad_out[0].astype(jnp.float32) * (conv_out + skip_row * mixed_f)).astype(
        jnp.bfloat16
    )
    mixed_grad = adjoint + skip_row * pulled_f
    grad_k_local = (mixed_grad * value_in[0].astype(jnp.float32)).astype(jnp.bfloat16)
    passing = (mixed_grad * gate_k[0].astype(jnp.float32)).astype(jnp.bfloat16)
    passed = shifted(passing[None], "section", -1)
    filter_local = (filter_corr * envelope).astype(jnp.bfloat16)
    rate_part = -jnp.sum(positions[:, None] * filter_corr * modulated, axis=0)
    skip_part = jnp.sum(mixed_f * pulled_f, axis=0)
    rate_total, skip_total = (
        lax.psum(rate_part.astype(jnp.bfloat16), "ctx").astype(jnp.float32),
        lax.psum(skip_part.astype(jnp.bfloat16), "ctx").astype(jnp.float32),
    )
    return (
        grad_q_local[None],
        grad_k_local[None],
        passed,
        filter_local[None],
        rate_total[None],
        skip_total[None],
    )


def solution(mesh):
    in_specs = (
        P("section", "ctx", None),
        P("section", "ctx", None),
        P("section", "ctx", None),
        P("section", "ctx", None),
        P("section", None),
        P("section", None),
        P("section", "ctx", None),
    )
    out_specs = (
        P("section", "ctx", None),
        P("section", "ctx", None),
        P("section", "ctx", None),
        P("section", "ctx", None),
        P("section", None),
        P("section", None),
    )
    return jax.shard_map(shards, mesh=mesh, in_specs=in_specs, out_specs=out_specs, check_vma=False)
```

profile of v0, /device:TPU:0, one launch (start us, length us, event | category | flops | bytes accessed | tf_op | source)
XLA Modules:
  0.0 480.3 jit_solution(238260348380390639)
XLA Ops:
  0.7 0.9 neg.39
  1.6 2.6 fusion.21
  4.2 5.2 %all-to-all-start = ((bf16[4,32,4096]{2,1,0:T(8,128)(2,1)}), bf16[4,32,4096]{2,1,0:T(8,128)(2,1)S(1)}, u32[]{:S(2)}, u32[]{:S(2)}) async-start(bf16[4,32,4096]{2,1,0:T(8,128)(2,1)} %fusion.21), calls=%async_computation | async-start | bytes 2097152 | tf_op jit(solution)/shard_map/all_to_all | solution.py:100
  9.4 3.6 fusion.19
  13.0 10.0 %all-to-all-done = bf16[4,32,4096]{2,1,0:T(8,128)(2,1)S(1)} async-done(((bf16[4,32,4096]{2,1,0:T(8,128)(2,1)}), bf16[4,32,4096]{2,1,0:T(8,128)(2,1)S(1)}, u32[]{:S(2)}, u32[]{:S(2)}) %all-to-all-start) | async-done | bytes 1048608 | tf_op jit(solution)/shard_map/all_to_all | solution.py:100
  23.0 3.5 all-to-all-start.6
  26.5 13.1 %all-to-all-done.6 = bf16[4,32,4096]{2,1,0:T(8,128)(2,1)S(1)} async-done(((bf16[4,32,4096]{2,1,0:T(8,128)(2,1)}), bf16[4,32,4096]{2,1,0:T(8,128)(2,1)S(1)}, u32[]{:S(2)}, u32[]{:S(2)}) %all-to-all-start.6) | async-done | bytes 1048608 | tf_op jit(solution)/shard_map/all_to_all | solution.py:103
  39.6 3.5 all-to-all-start.2
  43.2 6.4 %convolution_convert_fusion = bf16[2,2,4,32,4096]{4,2,3,1,0:T(4,128)(2,1)S(1)} fusion(bf16[4,32,4096,1,1]{2,1,0,4,3:T(8,128)(2,1)S(1)} %bitcast.132, f32[4,2,1,4]{0,3,2,1:T(4,128)S(1)} %get-tuple-element.33, f32[4,2,1,4]{0,3,2,1:T(4,128)S(1)} %get-tuple-element.32), kind=kOutput, calls=%fused_computation.15 | convolution fusion | flops 102760512 | bytes 5243136 | tf_op jit(solution)/shard_map/mgc,mlir->lirgc/dot_general | solution.py:108
  49.6 4.3 copy.56
  53.9 2.2 all-to-all-done.2
  56.2 5.0 %all-to-all-start.7 = ((bf16[2,2,4,32,4096]{4,3,1,0,2:T(8,128)(2,1)}), bf16[2,2,4,32,4096]{4,3,1,0,2:T(8,128)(2,1)}, u32[]{:S(2)}, u32[]{:S(2)}) async-start(bf16[2,2,4,32,4096]{4,3,1,0,2:T(8,128)(2,1)} %copy.56), calls=%async_computation.7 | async-start | bytes 8388608 | tf_op jit(solution)/shard_map/all_to_all | solution.py:119
  61.2 6.4 %convolution_convert_fusion.2 = bf16[2,2,4,32,4096]{4,2,3,1,0:T(4,128)(2,1)S(1)} fusion(bf16[4,32,4096,1,1]{2,1,0,4,3:T(8,128)(2,1)S(1)} %bitcast.128, f32[4,2,1,4]{0,3,2,1:T(4,128)S(1)} %get-tuple-element.33, f32[4,2,1,4]{0,3,2,1:T(4,128)S(1)} %get-tuple-element.32), kind=kOutput, calls=%fused_computation.17 | convolution fusion | flops 102760512 | bytes 5243136 | tf_op jit(solution)/shard_map/mgc,mlir->lirgc/dot_general | solution.py:108
  67.6 4.3 copy.44
  71.9 36.1 %all-to-all-done.7 = bf16[2,2,4,32,4096]{4,3,1,0,2:T(8,128)(2,1)} async-done(((bf16[2,2,4,32,4096]{4,3,1,0,2:T(8,128)(2,1)}), bf16[2,2,4,32,4096]{4,3,1,0,2:T(8,128)(2,1)}, u32[]{:S(2)}, u32[]{:S(2)}) %all-to-all-start.7) | async-done | bytes 4194336 | tf_op jit(solution)/shard_map/all_to_all | solution.py:119
  108.0 5.1 %all-to-all-start.1 = ((bf16[2,2,4,32,4096]{4,3,1,0,2:T(8,128)(2,1)}), bf16[2,2,4,32,4096]{4,3,1,0,2:T(8,128)(2,1)}, u32[]{:S(2)}, u32[]{:S(2)}) async-start(bf16[2,2,4,32,4096]{4,3,1,0,2:T(8,128)(2,1)} %copy.44), calls=%async_computation.1 | async-start | bytes 8388608 | tf_op jit(solution)/shard_map/all_to_all | solution.py:116
  113.1 6.4 %convolution_convert_fusion.1 = bf16[2,2,4,32,4096]{4,2,3,1,0:T(4,128)(2,1)S(1)} fusion(bf16[4,32,4096,1,1]{2,1,0,4,3:T(8,128)(2,1)S(1)} %bitcast.130, f32[4,2,1,4]{0,3,2,1:T(4,128)S(1)} %get-tuple-element.33, f32[4,2,1,4]{0,3,2,1:T(4,128)S(1)} %get-tuple-element.32), kind=kOutput, calls=%fused_computation.16 | convolution fusion | flops 102760512 | bytes 5243136 | tf_op jit(solution)/shard_map/mgc,mlir->lirgc/dot_general | solution.py:108
  119.5 4.3 copy.47
  123.8 36.2 %all-to-all-done.1 = bf16[2,2,4,32,4096]{4,3,1,0,2:T(8,128)(2,1)} async-done(((bf16[2,2,4,32,4096]{4,3,1,0,2:T(8,128)(2,1)}), bf16[2,2,4,32,4096]{4,3,1,0,2:T(8,128)(2,1)}, u32[]{:S(2)}, u32[]{:S(2)}) %all-to-all-start.1) | async-done | bytes 4194336 | tf_op jit(solution)/shard_map/all_to_all | solution.py:116
  160.0 5.3 %all-to-all-start.3 = ((bf16[2,2,4,32,4096]{4,3,1,0,2:T(8,128)(2,1)}), bf16[2,2,4,32,4096]{4,3,1,0,2:T(8,128)(2,1)}, u32[]{:S(2)}, u32[]{:S(2)}) async-start(bf16[2,2,4,32,4096]{4,3,1,0,2:T(8,128)(2,1)} %copy.47), calls=%async_computation.3 | async-start | bytes 8388608 | tf_op jit(solution)/shard_map/all_to_all | solution.py:113
  165.4 1.1 fusion.39
  166.6 2.5 copy.57
  169.1 2.5 copy.45
  171.5 5.6 %convolution_bitcast_fusion.2 = f32[2,2,128,4096]{3,2,1,0:T(8,128)} fusion(bf16[2,2,128,4096,1]{3,2,1,4,0:T(8,128)(2,1)S(1)} %bitcast.121, f32[2,1,128,2,128]{2,4,1,3,0:T(8,128)S(1)} %get-tuple-element.24, f32[2,1,128,2,128]{2,4,1,3,0:T(8,128)S(1)} %get-tuple-element.23), kind=kOutput, calls=%fused_computation.14 | convolution fusion | flops 6442582016 | bytes 13107200 | tf_op jit(solution)/shard_map/spjc,spjqb->sqbc/dot_general | solution.py:47
  177.1 5.7 %convolution_bitcast_fusion = f32[2,2,128,4096]{3,2,1,0:T(8,128)} fusion(bf16[2,2,128,4096,1]{3,2,1,4,0:T(8,128)(2,1)S(1)} %bitcast.119, f32[2,1,128,2,128]{2,4,1,3,0:T(8,128)S(1)} %get-tuple-element.24, f32[2,1,128,2,128]{2,4,1,3,0:T(8,128)S(1)} %get-tuple-element.23), kind=kOutput, calls=%fused_computation.12 | convolution fusion | flops 6442582016 | bytes 13107200 | tf_op jit(solution)/shard_map/spjc,spjqb->sqbc/dot_general | solution.py:47
  182.8 29.4 %all-to-all-done.3 = bf16[2,2,4,32,4096]{4,3,1,0,2:T(8,128)(2,1)} async-done(((bf16[2,2,4,32,4096]{4,3,1,0,2:T(8,128)(2,1)}), bf16[2,2,4,32,4096]{4,3,1,0,2:T(8,128)(2,1)}, u32[]{:S(2)}, u32[]{:S(2)}) %all-to-all-start.3) | async-done | bytes 4194336 | tf_op jit(solution)/shard_map/all_to_all | solution.py:113
  212.2 2.6 copy.48
  214.8 5.7 %convolution_bitcast_fusion.1 = f32[2,2,128,4096]{3,2,1,0:T(8,128)} fusion(bf16[2,2,128,4096,1]{3,2,1,4,0:T(8,128)(2,1)S(1)} %bitcast.120, f32[2,1,128,2,128]{2,4,1,3,0:T(8,128)S(1)} %get-tuple-element.24, f32[2,1,128,2,128]{2,4,1,3,0:T(8,128)S(1)} %get-tuple-element.23), kind=kOutput, calls=%fused_computation.13 | convolution fusion | flops 6442582016 | bytes 13107200 | tf_op jit(solution)/shard_map/spjc,spjqb->sqbc/dot_general | solution.py:47
  220.5 11.1 %multiply_add_fusion = (f32[2,1,128,4096]{3,2,1,0:T(8,128)S(1)}, f32[2,1,128,4096]{3,2,1,0:T(8,128)}, f32[2,1,128,4096]{3,2,1,0:T(8,128)}, f32[2,1,128,4096]{3,2,1,0:T(8,128)}) fusion(f32[2,2,128,4096]{3,2,1,0:T(8,128)} %convolution_bitcast_fusion, f32[2,2,128,4096]{3,2,1,0:T(8,128)} %convolution_bitcast_fusion.1, f32[2,2,128,4096]{3,2,1,0:T(8,128)S(1)} %bitcast.118), kind=kLoop, calls=%fused_computation.25 | loop fusion | flops 12582912 | bytes 41943040 | tf_op jit(solution)/shard_map/add | solution.py:70
  231.7 7.5 %maximum_bitcast_fusion = (f32[2,2,128,4096,1]{3,2,1,0,4:T(8,128)S(1)}, f32[2,2,128,4096,1]{3,2,1,0,4:T(8,128)}) fusion(f32[2,1,128,4096]{3,2,1,0:T(8,128)} %get-tuple-element.17, f32[2,1,128,4096]{3,2,1,0:T(8,128)} %get-tuple-element.18, f32[2,1,128,4096]{3,2,1,0:T(8,128)} %get-tuple-element.12, f32[2,1,128,4096]{3,2,1,0:T(8,128)S(1)} %get-tuple-element.11), kind=kLoop, calls=%fused_computation | loop fusion | flops 4194304 | bytes 33554432 | tf_op jit(solution)/shard_map/stack | solution.py:52
  239.2 8.0 %fusion.4 = bf16[2,2,128,4096,1]{3,2,1,0,4:T(8,128)(2,1)S(1)} fusion(f32[2,2,128,4096,1]{3,2,1,0,4:T(8,128)S(1)} %get-tuple-element.34, f32[2,1,128,2,128]{2,4,3,0,1:T(8,128)S(1)} %get-tuple-element.22, f32[2,1,128,2,128]{2,4,3,0,1:T(8,128)S(1)} %get-tuple-element.21), kind=kOutput, calls=%fused_computation.10 | convolution fusion | flops 6442582016 | bytes 13107200 | tf_op jit(solution)/shard_map/sqbc,sqbpj->spjc/dot_general | solution.py:53
  247.2 0.5 copy.136
  247.6 6.3 %copy.51 = bf16[2,2,4,32,4096]{4,0,1,3,2:T(2,128)(2,1)} copy(bf16[2,2,4,32,4096]{4,3,2,0,1:T(8,128)(2,1)S(1)} %bitcast.122) | data formatting | bytes 8388608 | tf_op jit(solution)/shard_map/reshape | solution.py:133
  254.0 5.1 %all-to-all-start.4 = ((bf16[2,2,4,32,4096]{4,0,1,3,2:T(2,128)(2,1)}), bf16[2,2,4,32,4096]{4,0,1,3,2:T(2,128)(2,1)}, u32[]{:S(2)}, u32[]{:S(2)}) async-start(bf16[2,2,4,32,4096]{4,0,1,3,2:T(2,128)(2,1)} %copy.51), calls=%async_computation.4 | async-start | bytes 8388608 | tf_op jit(solution)/shard_map/all_to_all | solution.py:136
  259.1 9.2 %fusion = bf16[2,2,128,4096,1]{3,2,1,0,4:T(8,128)(2,1)S(1)} fusion(f32[2,2,128,4096,1]{3,2,1,0,4:T(8,128)} %get-tuple-element.35, f32[2,1,128,2,128]{2,4,3,0,1:T(8,128)S(1)} %get-tuple-element.22, f32[2,1,128,2,128]{2,4,3,0,1:T(8,128)S(1)} %get-tuple-element.21), kind=kOutput, calls=%fused_computation.4 | convolution fusion | flops 6442582016 | bytes 13107200 | tf_op jit(solution)/shard_map/sqbc,sqbpj->spjc/dot_general | solution.py:53
  268.8 6.4 %copy.66 = bf16[2,2,4,32,4096]{4,0,1,3,2:T(2,128)(2,1)} copy(bf16[2,2,4,32,4096]{4,3,2,0,1:T(8,128)(2,1)S(1)} %bitcast.123) | data formatting | bytes 8388608 | tf_op jit(solution)/shard_map/reshape | solution.py:133
  275.2 30.8 %all-to-all-done.4 = bf16[2,2,4,32,4096]{4,0,1,3,2:T(2,128)(2,1)} async-done(((bf16[2,2,4,32,4096]{4,0,1,3,2:T(2,128)(2,1)}), bf16[2,2,4,32,4096]{4,0,1,3,2:T(2,128)(2,1)}, u32[]{:S(2)}, u32[]{:S(2)}) %all-to-all-start.4) | async-done | bytes 4194336 | tf_op jit(solution)/shard_map/all_to_all | solution.py:136
  306.0 5.1 %all-to-all-start.10 = ((bf16[2,2,4,32,4096]{4,0,1,3,2:T(2,128)(2,1)}), bf16[2,2,4,32,4096]{4,0,1,3,2:T(2,128)(2,1)}, u32[]{:S(2)}, u32[]{:S(2)}) async-start(bf16[2,2,4,32,4096]{4,0,1,3,2:T(2,128)(2,1)} %copy.66), calls=%async_computation.10 | async-start | bytes 8388608 | tf_op jit(solution)/shard_map/all_to_all | solution.py:138
  311.1 6.5 %multiply_add_fusion.1 = (f32[2,1,128,4096]{3,2,1,0:T(8,128)S(1)}, f32[2,1,128,4096]{3,2,1,0:T(8,128)S(1)}) fusion(f32[2,2,128,4096]{3,2,1,0:T(8,128)} %convolution_bitcast_fusion, f32[2,2,128,4096]{3,2,1,0:T(8,128)} %convolution_bitcast_fusion.2), kind=kLoop, calls=%fused_computation.27 | loop fusion | flops 6291456 | bytes 25165824 | tf_op jit(solution)/shard_map/add | solution.py:67
  317.7 7.8 %fusion.2 = bf16[2,2,128,4096,1]{3,2,1,0,4:T(8,128)(2,1)S(1)} fusion(f32[2,1,128,2,128]{2,4,3,0,1:T(8,128)S(1)} %get-tuple-element.22, f32[2,1,128,2,128]{2,4,3,0,1:T(8,128)S(1)} %get-tuple-element.21, f32[2,1,128,4096]{3,2,1,0:T(8,128)S(1)} %get-tuple-element.14, f32[2,1,128,4096]{3,2,1,0:T(8,128)S(1)} %get-tuple-element.13), kind=kOutput, calls=%fused_computation.7 | convolution fusion | flops 6444679168 | bytes 13107200 | tf_op jit(solution)/shard_map/sqbc,sqbpj->spjc/dot_general | solution.py:53
  326.0 6.3 %copy.60 = bf16[2,2,4,32,4096]{4,0,1,3,2:T(2,128)(2,1)} copy(bf16[2,2,4,32,4096]{4,3,2,0,1:T(8,128)(2,1)S(1)} %bitcast.124) | data formatting | bytes 8388608 | tf_op jit(solution)/shard_map/reshape | solution.py:133
  332.3 25.7 %all-to-all-done.10 = bf16[2,2,4,32,4096]{4,0,1,3,2:T(2,128)(2,1)} async-done(((bf16[2,2,4,32,4096]{4,0,1,3,2:T(2,128)(2,1)}), bf16[2,2,4,32,4096]{4,0,1,3,2:T(2,128)(2,1)}, u32[]{:S(2)}, u32[]{:S(2)}) %all-to-all-start.10) | async-done | bytes 4194336 | tf_op jit(solution)/shard_map/all_to_all | solution.py:138
  358.0 5.4 %all-to-all-start.8 = ((bf16[2,2,4,32,4096]{4,0,1,3,2:T(2,128)(2,1)}), bf16[2,2,4,32,4096]{4,0,1,3,2:T(2,128)(2,1)}, u32[]{:S(2)}, u32[]{:S(2)}) async-start(bf16[2,2,4,32,4096]{4,0,1,3,2:T(2,128)(2,1)} %copy.60), calls=%async_computation.8 | async-start | bytes 8388608 | tf_op jit(solution)/shard_map/all_to_all | solution.py:137
  363.4 10.8 %fusion.6 = bf16[4,32,4096]{2,0,1:T(4,128)(2,1)S(1)} fusion(bf16[2,2,4,32,4096]{4,0,1,3,2:T(2,128)(2,1)} %all-to-all-done.4, f32[4,2,1,4]{0,3,2,1:T(4,128)S(1)} %get-tuple-element.33, f32[4,2,1,4]{0,3,2,1:T(4,128)S(1)} %get-tuple-element.32), kind=kOutput, calls=%fused_computation.21 | convolution fusion | flops 101187712 | bytes 5243136 | tf_op jit(solution)/shard_map/lirgc,mlir->mgc/dot_general | solution.py:143
  374.2 1.6 copy.54
  375.7 34.5 %all-to-all-done.8 = bf16[2,2,4,32,4096]{4,0,1,3,2:T(2,128)(2,1)} async-done(((bf16[2,2,4,32,4096]{4,0,1,3,2:T(2,128)(2,1)}), bf16[2,2,4,32,4096]{4,0,1,3,2:T(2,128)(2,1)}, u32[]{:S(2)}, u32[]{:S(2)}) %all-to-all-start.8) | async-done | bytes 4194336 | tf_op jit(solution)/shard_map/all_to_all | solution.py:137
  410.2 3.5 all-to-all-start.5
  413.8 10.8 %fusion.7 = bf16[4,32,4096]{2,0,1:T(4,128)(2,1)S(1)} fusion(bf16[2,2,4,32,4096]{4,0,1,3,2:T(2,128)(2,1)} %all-to-all-done.8, f32[4,2,1,4]{0,3,2,1:T(4,128)S(1)} %get-tuple-element.33, f32[4,2,1,4]{0,3,2,1:T(4,128)S(1)} %get-tuple-element.32), kind=kOutput, calls=%fused_computation.22 | convolution fusion | flops 101187712 | bytes 5243136 | tf_op jit(solution)/shard_map/lirgc,mlir->mgc/dot_general | solution.py:143
  424.6 1.6 copy.63
  426.1 0.7 all-to-all-done.5
  426.9 3.7 all-to-all-start.9
  430.6 10.8 %fusion.8 = bf16[4,32,4096]{2,0,1:T(4,128)(2,1)S(1)} fusion(bf16[2,2,4,32,4096]{4,0,1,3,2:T(2,128)(2,1)} %all-to-all-done.10, f32[4,2,1,4]{0,3,2,1:T(4,128)S(1)} %get-tuple-element.33, f32[4,2,1,4]{0,3,2,1:T(4,128)S(1)} %get-tuple-element.32), kind=kOutput, calls=%fused_computation.23 | convolution fusion | flops 101187712 | bytes 5243136 | tf_op jit(solution)/shard_map/lirgc,mlir->mgc/dot_general | solution.py:143
  441.4 1.6 copy.69
  443.0 0.6 all-to-all-done.9
  443.6 3.6 all-to-all-start.11
  447.2 5.5 %fusion.14 = (bf16[1,128,4096]{2,1,0:T(8,128)(2,1)}, bf16[1,128,4096]{2,1,0:T(8,128)(2,1)}, bf16[1,128,4096]{2,1,0:T(8,128)(2,1)}) fusion(bf16[1,128,4096]{2,1,0:T(8,128)(2,1)} %param.8, bf16[1,128,4096]{2,1,0:T(8,128)(2,1)} %get-tuple-element.9, f32[4096]{0:T(1024)S(1)} %bitcast.136, bf16[1,128,4096]{2,1,0:T(8,128)(2,1)} %param.9, ...), kind=kLoop, calls=%fused_computation.43 | loop fusion | flops 8912896 | bytes 10502144 | tf_op jit(solution)/shard_map/convert_element_type | solution.py:162
  452.7 1.3 collective-permute-start
  454.0 6.2 %all-to-all-done.11 = bf16[4,32,4096]{2,1,0:T(8,128)(2,1)S(1)} async-done(((bf16[4,32,4096]{2,1,0:T(8,128)(2,1)}), bf16[4,32,4096]{2,1,0:T(8,128)(2,1)S(1)}, u32[]{:S(2)}, u32[]{:S(2)}) %all-to-all-start.11) | async-done | bytes 1048608 | tf_op jit(solution)/shard_map/all_to_all | solution.py:150
  460.2 0.7 multiply_reduce_fusion
  461.0 15.3 %all-reduce = (bf16[1,4096]{1,0:T(2,128)(2,1)S(1)}, bf16[1,4096]{1,0:T(2,128)(2,1)S(1)}) all-reduce(bf16[1,4096]{1,0:T(2,128)(2,1)S(1)} %broadcast_in_dim.10, bf16[1,4096]{1,0:T(2,128)(2,1)S(1)} %broadcast_in_dim.12), channel_id=1, replica_groups=mesh['section'=8,'ctx'=4] {'ctx'}, use_global_device_ids=true, to_apply=%region_1.2 | all-reduce | flops 8192 | bytes 32768 | tf_op jit(solution)/shard_map/psum | solution.py:168
  476.3 0.6 broadcast_in_dim.11
  476.9 0.6 broadcast_in_dim.13
  477.8 1.4 fusion.20
  479.1 1.0 copy.138
  (31 shorter events, 1.5 us)
Async XLA Ops:
  0.6 8.7 %copy-start.3 = (bf16[1,128,4096]{2,1,0:T(8,128)(2,1)S(1)}, bf16[1,128,4096]{2,1,0:T(8,128)(2,1)}, u32[]{:S(2)}) copy-start(bf16[1,128,4096]{2,1,0:T(8,128)(2,1)} %param.13) | copy-start | bytes 3145732
  0.6 8.7 %copy-start.2 = (bf16[1,128,4096]{2,1,0:T(8,128)(2,1)S(1)}, bf16[1,128,4096]{2,1,0:T(8,128)(2,1)}, u32[]{:S(2)}) copy-start(bf16[1,128,4096]{2,1,0:T(8,128)(2,1)} %param.8) | copy-start | bytes 3145732
  4.2 18.8 %all-to-all-start = ((bf16[4,32,4096]{2,1,0:T(8,128)(2,1)}), bf16[4,32,4096]{2,1,0:T(8,128)(2,1)S(1)}, u32[]{:S(2)}, u32[]{:S(2)}) async-start(bf16[4,32,4096]{2,1,0:T(8,128)(2,1)} %fusion.21), calls=%async_computation | async-start | bytes 2097152 | tf_op jit(solution)/shard_map/all_to_all | solution.py:100
  23.0 16.6 %all-to-all-start.6 = ((bf16[4,32,4096]{2,1,0:T(8,128)(2,1)}), bf16[4,32,4096]{2,1,0:T(8,128)(2,1)S(1)}, u32[]{:S(2)}, u32[]{:S(2)}) async-start(bf16[4,32,4096]{2,1,0:T(8,128)(2,1)} %bitcast.32), calls=%async_computation.6 | async-start | bytes 2097152 | tf_op jit(solution)/shard_map/all_to_all | solution.py:103
  39.6 16.6 %all-to-all-start.2 = ((bf16[4,32,4096]{2,1,0:T(8,128)(2,1)}), bf16[4,32,4096]{2,1,0:T(8,128)(2,1)S(1)}, u32[]{:S(2)}, u32[]{:S(2)}) async-start(bf16[4,32,4096]{2,1,0:T(8,128)(2,1)} %bitcast.17), calls=%async_computation.2 | async-start | bytes 2097152 | tf_op jit(solution)/shard_map/all_to_all | solution.py:97
  56.2 51.9 %all-to-all-start.7 = ((bf16[2,2,4,32,4096]{4,3,1,0,2:T(8,128)(2,1)}), bf16[2,2,4,32,4096]{4,3,1,0,2:T(8,128)(2,1)}, u32[]{:S(2)}, u32[]{:S(2)}) async-start(bf16[2,2,4,32,4096]{4,3,1,0,2:T(8,128)(2,1)} %copy.56), calls=%async_computation.7 | async-start | bytes 8388608 | tf_op jit(solution)/shard_map/all_to_all | solution.py:119
  108.0 52.0 %all-to-all-start.1 = ((bf16[2,2,4,32,4096]{4,3,1,0,2:T(8,128)(2,1)}), bf16[2,2,4,32,4096]{4,3,1,0,2:T(8,128)(2,1)}, u32[]{:S(2)}, u32[]{:S(2)}) async-start(bf16[2,2,4,32,4096]{4,3,1,0,2:T(8,128)(2,1)} %copy.44), calls=%async_computation.1 | async-start | bytes 8388608 | tf_op jit(solution)/shard_map/all_to_all | solution.py:116
  160.0 52.2 %all-to-all-start.3 = ((bf16[2,2,4,32,4096]{4,3,1,0,2:T(8,128)(2,1)}), bf16[2,2,4,32,4096]{4,3,1,0,2:T(8,128)(2,1)}, u32[]{:S(2)}, u32[]{:S(2)}) async-start(bf16[2,2,4,32,4096]{4,3,1,0,2:T(8,128)(2,1)} %copy.47), calls=%async_computation.3 | async-start | bytes 8388608 | tf_op jit(solution)/shard_map/all_to_all | solution.py:113
  212.2 8.3 %slice-start = ((s8[8388608]{0:T(1024)(128)(4,1)}), s8[4194304]{0:T(1024)(128)(4,1)S(1)}, s32[]{:S(2)}) async-start(s8[8388608]{0:T(1024)(128)(4,1)} %bitcast.117), calls=%async_computation.12 | async-start | bytes 8388608
  214.8 5.7 %slice-start.1 = ((s8[8388608]{0:T(1024)(128)(4,1)}), s8[4194304]{0:T(1024)(128)(4,1)S(1)}, s32[]{:S(2)}) async-start(s8[8388608]{0:T(1024)(128)(4,1)} %bitcast.117), calls=%async_computation.13 | async-start | bytes 8388608
  254.0 52.0 %all-to-all-start.4 = ((bf16[2,2,4,32,4096]{4,0,1,3,2:T(2,128)(2,1)}), bf16[2,2,4,32,4096]{4,0,1,3,2:T(2,128)(2,1)}, u32[]{:S(2)}, u32[]{:S(2)}) async-start(bf16[2,2,4,32,4096]{4,0,1,3,2:T(2,128)(2,1)} %copy.51), calls=%async_computation.4 | async-start | bytes 8388608 | tf_op jit(solution)/shard_map/all_to_all | solution.py:136
  306.0 52.0 %all-to-all-start.10 = ((bf16[2,2,4,32,4096]{4,0,1,3,2:T(2,128)(2,1)}), bf16[2,2,4,32,4096]{4,0,1,3,2:T(2,128)(2,1)}, u32[]{:S(2)}, u32[]{:S(2)}) async-start(bf16[2,2,4,32,4096]{4,0,1,3,2:T(2,128)(2,1)} %copy.66), calls=%async_computation.10 | async-start | bytes 8388608 | tf_op jit(solution)/shard_map/all_to_all | solution.py:138
  358.0 52.3 %all-to-all-start.8 = ((bf16[2,2,4,32,4096]{4,0,1,3,2:T(2,128)(2,1)}), bf16[2,2,4,32,4096]{4,0,1,3,2:T(2,128)(2,1)}, u32[]{:S(2)}, u32[]{:S(2)}) async-start(bf16[2,2,4,32,4096]{4,0,1,3,2:T(2,128)(2,1)} %copy.60), calls=%async_computation.8 | async-start | bytes 8388608 | tf_op jit(solution)/shard_map/all_to_all | solution.py:137
  410.2 16.6 %all-to-all-start.5 = ((bf16[4,32,4096]{2,1,0:T(8,128)(2,1)}), bf16[4,32,4096]{2,1,0:T(8,128)(2,1)S(1)}, u32[]{:S(2)}, u32[]{:S(2)}) async-start(bf16[4,32,4096]{2,1,0:T(8,128)(2,1)} %copy.54), calls=%async_computation.5 | async-start | bytes 2097152 | tf_op jit(solution)/shard_map/all_to_all | solution.py:148
  426.9 16.7 %all-to-all-start.9 = ((bf16[4,32,4096]{2,1,0:T(8,128)(2,1)}), bf16[4,32,4096]{2,1,0:T(8,128)(2,1)S(1)}, u32[]{:S(2)}, u32[]{:S(2)}) async-start(bf16[4,32,4096]{2,1,0:T(8,128)(2,1)} %copy.63), calls=%async_computation.9 | async-start | bytes 2097152 | tf_op jit(solution)/shard_map/all_to_all | solution.py:149
  441.4 5.7 %copy-start.4 = (f32[1,4096]{1,0:T(1,128)S(1)}, f32[1,4096]{1,0:T(1,128)}, u32[]{:S(2)}) copy-start(f32[1,4096]{1,0:T(1,128)} %param.12) | copy-start | bytes 49156
  443.6 3.6 copy-start.1
  443.6 16.6 %all-to-all-start.11 = ((bf16[4,32,4096]{2,1,0:T(8,128)(2,1)}), bf16[4,32,4096]{2,1,0:T(8,128)(2,1)S(1)}, u32[]{:S(2)}, u32[]{:S(2)}) async-start(bf16[4,32,4096]{2,1,0:T(8,128)(2,1)} %copy.69), calls=%async_computation.11 | async-start | bytes 2097152 | tf_op jit(solution)/shard_map/all_to_all | solution.py:150
  447.2 13.0 %copy-start = (bf16[1,128,4096]{2,1,0:T(8,128)(2,1)S(1)}, bf16[1,128,4096]{2,1,0:T(8,128)(2,1)}, u32[]{:S(2)}) copy-start(bf16[1,128,4096]{2,1,0:T(8,128)(2,1)} %param.10) | copy-start | bytes 3145732
  452.7 26.4 %collective-permute-start = (bf16[1,128,4096]{2,1,0:T(8,128)(2,1)}, bf16[1,128,4096]{2,1,0:T(8,128)(2,1)S(1)}, u32[]{:S(2)}, u32[]{:S(2)}) collective-permute-start(bf16[1,128,4096]{2,1,0:T(8,128)(2,1)} %get-tuple-element.19), channel_id=1, source_target_pairs={{4,0},{8,4},{12,8},{16,12},{20,16},{24,20},{28,24},{5,1},{9,5},{13... | collective-permute-start | bytes 3145736 | tf_op jit(solution)/shard_map/ppermute | solution.py:13
where the time goes:
time: 489 us; the launch traced here: 480 us
  waiting for transfers between devices  226 us (46%)
  matrix products  93.4 us (19%)
  starting transfers between devices  55.3 us (11%)
  local copies, waits for them, and re-layouts  46.6 us (10%)
  other arithmetic  42.8 us (9%)
  blocking collectives  15.3 us (3%)
    all_to_all x1, waiting for transfers between devices, shards(): lax.all_to_all(first_section(sectioned_filter), 'ctx', split_axis=2, conc...  36.2 us
    all_to_all x1, waiting for transfers between devices, shards(): lax.all_to_all(first_section(sectioned_pulled), 'ctx', split_axis=2, conc...  36.1 us
    all_to_all x1, waiting for transfers between devices, shards(): lax.all_to_all(pack(folded_adj), 'ctx', split_axis=2, concat_axis=2, tile...  34.5 us
    dot_general x3, matrix products, last_section(): jnp.einsum('lirgc,mlir->mgc', received.astype(jnp.float32), table_last, p...  32.4 us
    all_to_all x1, waiting for transfers between devices, shards(): lax.all_to_all(pack(folded_conv), 'ctx', split_axis=2, concat_axis=2, til...  30.8 us
    all_to_all x1, waiting for transfers between devices, shards(): lax.all_to_all(first_section(sectioned_mixed), 'ctx', split_axis=2, conca...  29.4 us
    all_to_all x1, waiting for transfers between devices, shards(): lax.all_to_all(pack(folded_cor), 'ctx', split_axis=2, concat_axis=2, tile...  25.7 us
    dot_general x3, matrix products, inverse(): jnp.einsum('sqbc,sqbpj->spjc', stacked, inverse_table, precision=exact_mode)  25 us
  transfers between devices with their start and end apart: 13, of which 12 were waited for; matrix products, arithmetic and copies ran while one was open for 28% of the time, Pallas kernels for 0%

commit v1 on v0

--- a/solution.py
+++ b/solution.py
@@ -133,7 +133,12 @@
         return folded.reshape(2, 2, parts_count, group_rows, channels)
 
     back_conv, back_adj, back_cor = (
-        lax.all_to_all(pack(folded_conv), "ctx", split_axis=2, concat_axis=2, tiled=True),
+        jnp.concatenate(
+            lax.all_to_all(
+                jnp.stack(jnp.split(pack(folded_conv), lax.axis_size("ctx"), axis=2)), "ctx", 0, 0
+            ),
+            axis=2,
+        ),
         lax.all_to_all(pack(folded_adj), "ctx", split_axis=2, concat_axis=2, tiled=True),
         lax.all_to_all(pack(folded_cor), "ctx", split_axis=2, concat_axis=2, tiled=True),
     )

time: 489 us -> 489 us (level)
    another operation x0 -> x1, local copies, waits for them, and re-layouts: none -> 6.38 us  [shards(): jnp.stack(jnp.split(pack(folded_conv), lax.axis_size('ctx'), axis=2))]
    reshape x3 -> x2, local copies, waits for them, and re-layouts: 19.1 us -> 12.8 us  [pack(): return folded.reshape(2, 2, parts_count, group_rows, channels)]
    all_to_all x1, waiting for transfers between devices: 34.5 us -> 29.6 us  [shards(): lax.all_to_all(pack(folded_adj), 'ctx', split_axis=2, concat_axis=2, tile...]
  transfers between devices with their start and end apart: 13 -> 13, of which waited for: 12 -> 12; matrix products, arithmetic and copies ran while one was open for 28% -> 29% of each run, Pallas kernels for 0% -> 0%
where the time goes in v1:
time: 489 us; the launch traced here: 480 us
  waiting for transfers between devices  224 us (46%)
  matrix products  93.5 us (19%)
  starting transfers between devices  55.2 us (11%)
  local copies, waits for them, and re-layouts  47.3 us (10%)
  other arithmetic  43.4 us (9%)
  blocking collectives  15.3 us (3%)
    all_to_all x1, waiting for transfers between devices, shards(): lax.all_to_all(first_section(sectioned_filter), 'ctx', split_axis=2, conc...  36.2 us
    all_to_all x1, waiting for transfers between devices, shards(): lax.all_to_all(first_section(sectioned_pulled), 'ctx', split_axis=2, conc...  36.1 us
    all_to_all x1, waiting for transfers between devices, shards(): lax.all_to_all(jnp.stack(jnp.split(pack(folded_conv), lax.axis_size('ctx'...  34.5 us
    dot_general x3, matrix products, last_section(): jnp.einsum('lirgc,mlir->mgc', received.astype(jnp.float32), table_last, p...  32.4 us
    all_to_all x1, waiting for transfers between devices, shards(): lax.all_to_all(pack(folded_adj), 'ctx', split_axis=2, concat_axis=2, tile...  29.6 us
    all_to_all x1, waiting for transfers between devices, shards(): lax.all_to_all(first_section(sectioned_mixed), 'ctx', split_axis=2, conca...  29.4 us
    all_to_all x1, waiting for transfers between devices, shards(): lax.all_to_all(pack(folded_cor), 'ctx', split_axis=2, concat_axis=2, tile...  25.6 us
    dot_general x3, matrix products, inverse(): jnp.einsum('sqbc,sqbpj->spjc', stacked, inverse_table, precision=exact_mode)  25 us
  transfers between devices with their start and end apart: 13, of which 12 were waited for; matrix products, arithmetic and copies ran while one was open for 29% of the time, Pallas kernels for 0%

profile of v1, /device:TPU:0, one launch (start us, length us, event | category | flops | bytes accessed | tf_op | source)
XLA Modules:
  0.0 480.3 jit_solution(15390053669320951833)
XLA Ops:
  0.7 0.9 neg.39
  1.6 2.6 fusion.22
  4.2 5.2 %all-to-all-start = ((bf16[4,32,4096]{2,1,0:T(8,128)(2,1)}), bf16[4,32,4096]{2,1,0:T(8,128)(2,1)S(1)}, u32[]{:S(2)}, u32[]{:S(2)}) async-start(bf16[4,32,4096]{2,1,0:T(8,128)(2,1)} %fusion.22), calls=%async_computation | async-start | bytes 2097152 | tf_op jit(solution)/shard_map/all_to_all | solution.py:100
  9.4 3.6 fusion.20
  13.0 10.0 %all-to-all-done = bf16[4,32,4096]{2,1,0:T(8,128)(2,1)S(1)} async-done(((bf16[4,32,4096]{2,1,0:T(8,128)(2,1)}), bf16[4,32,4096]{2,1,0:T(8,128)(2,1)S(1)}, u32[]{:S(2)}, u32[]{:S(2)}) %all-to-all-start) | async-done | bytes 1048608 | tf_op jit(solution)/shard_map/all_to_all | solution.py:100
  23.0 3.5 all-to-all-start.6
  26.5 13.1 %all-to-all-done.6 = bf16[4,32,4096]{2,1,0:T(8,128)(2,1)S(1)} async-done(((bf16[4,32,4096]{2,1,0:T(8,128)(2,1)}), bf16[4,32,4096]{2,1,0:T(8,128)(2,1)S(1)}, u32[]{:S(2)}, u32[]{:S(2)}) %all-to-all-start.6) | async-done | bytes 1048608 | tf_op jit(solution)/shard_map/all_to_all | solution.py:103
  39.6 3.5 all-to-all-start.2
  43.2 6.4 %convolution_convert_fusion = bf16[2,2,4,32,4096]{4,2,3,1,0:T(4,128)(2,1)S(1)} fusion(bf16[4,32,4096,1,1]{2,1,0,4,3:T(8,128)(2,1)S(1)} %bitcast.149, f32[4,2,1,4]{0,3,2,1:T(4,128)S(1)} %get-tuple-element.37, f32[4,2,1,4]{0,3,2,1:T(4,128)S(1)} %get-tuple-element.36), kind=kOutput, calls=%fused_computation.15 | convolution fusion | flops 102760512 | bytes 5243136 | tf_op jit(solution)/shard_map/mgc,mlir->lirgc/dot_general | solution.py:108
  49.6 4.3 copy.70
  53.9 2.2 all-to-all-done.2
  56.2 5.0 %all-to-all-start.7 = ((bf16[2,2,4,32,4096]{4,3,1,0,2:T(8,128)(2,1)}), bf16[2,2,4,32,4096]{4,3,1,0,2:T(8,128)(2,1)}, u32[]{:S(2)}, u32[]{:S(2)}) async-start(bf16[2,2,4,32,4096]{4,3,1,0,2:T(8,128)(2,1)} %copy.70), calls=%async_computation.7 | async-start | bytes 8388608 | tf_op jit(solution)/shard_map/all_to_all | solution.py:119
  61.2 6.4 %convolution_convert_fusion.2 = bf16[2,2,4,32,4096]{4,2,3,1,0:T(4,128)(2,1)S(1)} fusion(bf16[4,32,4096,1,1]{2,1,0,4,3:T(8,128)(2,1)S(1)} %bitcast.145, f32[4,2,1,4]{0,3,2,1:T(4,128)S(1)} %get-tuple-element.37, f32[4,2,1,4]{0,3,2,1:T(4,128)S(1)} %get-tuple-element.36), kind=kOutput, calls=%fused_computation.17 | convolution fusion | flops 102760512 | bytes 5243136 | tf_op jit(solution)/shard_map/mgc,mlir->lirgc/dot_general | solution.py:108
  67.6 4.3 copy.54
  71.9 36.1 %all-to-all-done.7 = bf16[2,2,4,32,4096]{4,3,1,0,2:T(8,128)(2,1)} async-done(((bf16[2,2,4,32,4096]{4,3,1,0,2:T(8,128)(2,1)}), bf16[2,2,4,32,4096]{4,3,1,0,2:T(8,128)(2,1)}, u32[]{:S(2)}, u32[]{:S(2)}) %all-to-all-start.7) | async-done | bytes 4194336 | tf_op jit(solution)/shard_map/all_to_all | solution.py:119
  108.0 5.1 %all-to-all-start.1 = ((bf16[2,2,4,32,4096]{4,3,1,0,2:T(8,128)(2,1)}), bf16[2,2,4,32,4096]{4,3,1,0,2:T(8,128)(2,1)}, u32[]{:S(2)}, u32[]{:S(2)}) async-start(bf16[2,2,4,32,4096]{4,3,1,0,2:T(8,128)(2,1)} %copy.54), calls=%async_computation.1 | async-start | bytes 8388608 | tf_op jit(solution)/shard_map/all_to_all | solution.py:116
  113.1 6.4 %convolution_convert_fusion.1 = bf16[2,2,4,32,4096]{4,2,3,1,0:T(4,128)(2,1)S(1)} fusion(bf16[4,32,4096,1,1]{2,1,0,4,3:T(8,128)(2,1)S(1)} %bitcast.147, f32[4,2,1,4]{0,3,2,1:T(4,128)S(1)} %get-tuple-element.37, f32[4,2,1,4]{0,3,2,1:T(4,128)S(1)} %get-tuple-element.36), kind=kOutput, calls=%fused_computation.16 | convolution fusion | flops 102760512 | bytes 5243136 | tf_op jit(solution)/shard_map/mgc,mlir->lirgc/dot_general | solution.py:108
  119.5 4.3 copy.57
  123.8 36.2 %all-to-all-done.1 = bf16[2,2,4,32,4096]{4,3,1,0,2:T(8,128)(2,1)} async-done(((bf16[2,2,4,32,4096]{4,3,1,0,2:T(8,128)(2,1)}), bf16[2,2,4,32,4096]{4,3,1,0,2:T(8,128)(2,1)}, u32[]{:S(2)}, u32[]{:S(2)}) %all-to-all-start.1) | async-done | bytes 4194336 | tf_op jit(solution)/shard_map/all_to_all | solution.py:116
  160.0 5.3 %all-to-all-start.3 = ((bf16[2,2,4,32,4096]{4,3,1,0,2:T(8,128)(2,1)}), bf16[2,2,4,32,4096]{4,3,1,0,2:T(8,128)(2,1)}, u32[]{:S(2)}, u32[]{:S(2)}) async-start(bf16[2,2,4,32,4096]{4,3,1,0,2:T(8,128)(2,1)} %copy.57), calls=%async_computation.3 | async-start | bytes 8388608 | tf_op jit(solution)/shard_map/all_to_all | solution.py:113
  165.4 1.1 fusion.40
  166.6 2.5 copy.71
  169.1 2.5 copy.55
  171.5 5.6 %convolution_bitcast_fusion.2 = f32[2,2,128,4096]{3,2,1,0:T(8,128)} fusion(bf16[2,2,128,4096,1]{3,2,1,4,0:T(8,128)(2,1)S(1)} %bitcast.138, f32[2,1,128,2,128]{2,4,1,3,0:T(8,128)S(1)} %get-tuple-element.28, f32[2,1,128,2,128]{2,4,1,3,0:T(8,128)S(1)} %get-tuple-element.27), kind=kOutput, calls=%fused_computation.14 | convolution fusion | flops 6442582016 | bytes 13107200 | tf_op jit(solution)/shard_map/spjc,spjqb->sqbc/dot_general | solution.py:47
  177.1 5.7 %convolution_bitcast_fusion = f32[2,2,128,4096]{3,2,1,0:T(8,128)} fusion(bf16[2,2,128,4096,1]{3,2,1,4,0:T(8,128)(2,1)S(1)} %bitcast.136, f32[2,1,128,2,128]{2,4,1,3,0:T(8,128)S(1)} %get-tuple-element.28, f32[2,1,128,2,128]{2,4,1,3,0:T(8,128)S(1)} %get-tuple-element.27), kind=kOutput, calls=%fused_computation.12 | convolution fusion | flops 6442582016 | bytes 13107200 | tf_op jit(solution)/shard_map/spjc,spjqb->sqbc/dot_general | solution.py:47
  182.8 29.4 %all-to-all-done.3 = bf16[2,2,4,32,4096]{4,3,1,0,2:T(8,128)(2,1)} async-done(((bf16[2,2,4,32,4096]{4,3,1,0,2:T(8,128)(2,1)}), bf16[2,2,4,32,4096]{4,3,1,0,2:T(8,128)(2,1)}, u32[]{:S(2)}, u32[]{:S(2)}) %all-to-all-start.3) | async-done | bytes 4194336 | tf_op jit(solution)/shard_map/all_to_all | solution.py:113
  212.2 2.6 copy.58
  214.8 5.7 %convolution_bitcast_fusion.1 = f32[2,2,128,4096]{3,2,1,0:T(8,128)} fusion(bf16[2,2,128,4096,1]{3,2,1,4,0:T(8,128)(2,1)S(1)} %bitcast.137, f32[2,1,128,2,128]{2,4,1,3,0:T(8,128)S(1)} %get-tuple-element.28, f32[2,1,128,2,128]{2,4,1,3,0:T(8,128)S(1)} %get-tuple-element.27), kind=kOutput, calls=%fused_computation.13 | convolution fusion | flops 6442582016 | bytes 13107200 | tf_op jit(solution)/shard_map/spjc,spjqb->sqbc/dot_general | solution.py:47
  220.5 11.1 %multiply_add_fusion = (f32[2,1,128,4096]{3,2,1,0:T(8,128)S(1)}, f32[2,1,128,4096]{3,2,1,0:T(8,128)}, f32[2,1,128,4096]{3,2,1,0:T(8,128)}, f32[2,1,128,4096]{3,2,1,0:T(8,128)}) fusion(f32[2,2,128,4096]{3,2,1,0:T(8,128)} %convolution_bitcast_fusion, f32[2,2,128,4096]{3,2,1,0:T(8,128)} %convolution_bitcast_fusion.1, f32[2,2,128,4096]{3,2,1,0:T(8,128)S(1)} %bitcast.135), kind=kLoop, calls=%fused_computation.28 | loop fusion | flops 12582912 | bytes 41943040 | tf_op jit(solution)/shard_map/add | solution.py:70
  231.6 7.5 %maximum_bitcast_fusion = (f32[2,2,128,4096,1]{3,2,1,0,4:T(8,128)}, f32[2,2,128,4096,1]{3,2,1,0,4:T(8,128)S(1)}) fusion(f32[2,1,128,4096]{3,2,1,0:T(8,128)} %get-tuple-element.17, f32[2,1,128,4096]{3,2,1,0:T(8,128)} %get-tuple-element.18, f32[2,1,128,4096]{3,2,1,0:T(8,128)} %get-tuple-element.12, f32[2,1,128,4096]{3,2,1,0:T(8,128)S(1)} %get-tuple-element.11), kind=kLoop, calls=%fused_computation | loop fusion | flops 4194304 | bytes 33554432 | tf_op jit(solution)/shard_map/stack | solution.py:52
  239.2 8.0 %fusion = bf16[2,2,128,4096,1]{3,2,1,0,4:T(8,128)(2,1)S(1)} fusion(f32[2,2,128,4096,1]{3,2,1,0,4:T(8,128)S(1)} %get-tuple-element.39, f32[2,1,128,2,128]{2,4,3,0,1:T(8,128)S(1)} %get-tuple-element.26, f32[2,1,128,2,128]{2,4,3,0,1:T(8,128)S(1)} %get-tuple-element.25), kind=kOutput, calls=%fused_computation.4 | convolution fusion | flops 6442582016 | bytes 13107200 | tf_op jit(solution)/shard_map/sqbc,sqbpj->spjc/dot_general | solution.py:53
  247.7 6.4 %copy.80 = bf16[2,2,4,32,4096]{4,0,1,3,2:T(2,128)(2,1)} copy(bf16[2,2,4,32,4096]{4,3,2,0,1:T(8,128)(2,1)S(1)} %bitcast.140) | data formatting | bytes 8388608 | tf_op jit(solution)/shard_map/reshape | solution.py:133
  254.0 5.1 %all-to-all-start.10 = ((bf16[2,2,4,32,4096]{4,0,1,3,2:T(2,128)(2,1)}), bf16[2,2,4,32,4096]{4,0,1,3,2:T(2,128)(2,1)}, u32[]{:S(2)}, u32[]{:S(2)}) async-start(bf16[2,2,4,32,4096]{4,0,1,3,2:T(2,128)(2,1)} %copy.80), calls=%async_computation.10 | async-start | bytes 8388608 | tf_op jit(solution)/shard_map/all_to_all | solution.py:143
  259.1 6.5 %multiply_add_fusion.1 = (f32[2,1,128,4096]{3,2,1,0:T(8,128)S(1)}, f32[2,1,128,4096]{3,2,1,0:T(8,128)S(1)}) fusion(f32[2,2,128,4096]{3,2,1,0:T(8,128)} %convolution_bitcast_fusion, f32[2,2,128,4096]{3,2,1,0:T(8,128)} %convolution_bitcast_fusion.2), kind=kLoop, calls=%fused_computation.30 | loop fusion | flops 6291456 | bytes 25165824 | tf_op jit(solution)/shard_map/add | solution.py:67
  265.7 7.8 %fusion.2 = bf16[2,2,128,4096,1]{3,2,1,0,4:T(8,128)(2,1)S(1)} fusion(f32[2,1,128,2,128]{2,4,3,0,1:T(8,128)S(1)} %get-tuple-element.26, f32[2,1,128,2,128]{2,4,3,0,1:T(8,128)S(1)} %get-tuple-element.25, f32[2,1,128,4096]{3,2,1,0:T(8,128)S(1)} %get-tuple-element.14, f32[2,1,128,4096]{3,2,1,0:T(8,128)S(1)} %get-tuple-element.13), kind=kOutput, calls=%fused_computation.7 | convolution fusion | flops 6444679168 | bytes 13107200 | tf_op jit(solution)/shard_map/sqbc,sqbpj->spjc/dot_general | solution.py:53
  274.0 6.4 %copy.74 = bf16[2,2,4,32,4096]{4,0,1,3,2:T(2,128)(2,1)} copy(bf16[2,2,4,32,4096]{4,3,2,0,1:T(8,128)(2,1)S(1)} %bitcast.141) | data formatting | bytes 8388608 | tf_op jit(solution)/shard_map/reshape | solution.py:133
  280.4 25.6 %all-to-all-done.10 = bf16[2,2,4,32,4096]{4,0,1,3,2:T(2,128)(2,1)} async-done(((bf16[2,2,4,32,4096]{4,0,1,3,2:T(2,128)(2,1)}), bf16[2,2,4,32,4096]{4,0,1,3,2:T(2,128)(2,1)}, u32[]{:S(2)}, u32[]{:S(2)}) %all-to-all-start.10) | async-done | bytes 4194336 | tf_op jit(solution)/shard_map/all_to_all | solution.py:143
  306.0 5.1 %all-to-all-start.8 = ((bf16[2,2,4,32,4096]{4,0,1,3,2:T(2,128)(2,1)}), bf16[2,2,4,32,4096]{4,0,1,3,2:T(2,128)(2,1)}, u32[]{:S(2)}, u32[]{:S(2)}) async-start(bf16[2,2,4,32,4096]{4,0,1,3,2:T(2,128)(2,1)} %copy.74), calls=%async_computation.8 | async-start | bytes 8388608 | tf_op jit(solution)/shard_map/all_to_all | solution.py:142
  311.1 9.2 %fusion.4 = bf16[2,2,128,4096,1]{3,2,1,0,4:T(8,128)(2,1)S(1)} fusion(f32[2,2,128,4096,1]{3,2,1,0,4:T(8,128)} %get-tuple-element.38, f32[2,1,128,2,128]{2,4,3,0,1:T(8,128)S(1)} %get-tuple-element.26, f32[2,1,128,2,128]{2,4,3,0,1:T(8,128)S(1)} %get-tuple-element.25), kind=kOutput, calls=%fused_computation.10 | convolution fusion | flops 6442582016 | bytes 13107200 | tf_op jit(solution)/shard_map/sqbc,sqbpj->spjc/dot_general | solution.py:53
  321.4 0.6 pad_maximum_fusion
  322.0 6.4 %copy.65 = bf16[4,2,2,1,32,4096]{5,1,2,4,3,0:T(2,128)(2,1)} copy(bf16[4,2,2,1,32,4096]{5,4,2,1,3,0:T(8,128)(2,1)S(1)} %pad_maximum_fusion) | data formatting | bytes 8388608 | tf_op jit(solution)/shard_map/stack | solution.py:138
  328.4 29.6 %all-to-all-done.8 = bf16[2,2,4,32,4096]{4,0,1,3,2:T(2,128)(2,1)} async-done(((bf16[2,2,4,32,4096]{4,0,1,3,2:T(2,128)(2,1)}), bf16[2,2,4,32,4096]{4,0,1,3,2:T(2,128)(2,1)}, u32[]{:S(2)}, u32[]{:S(2)}) %all-to-all-start.8) | async-done | bytes 4194336 | tf_op jit(solution)/shard_map/all_to_all | solution.py:142
  358.0 5.4 %all-to-all-start.4 = ((bf16[4,2,2,1,32,4096]{5,1,2,4,3,0:T(2,128)(2,1)}), bf16[4,2,2,1,32,4096]{5,1,2,4,3,0:T(2,128)(2,1)}, u32[]{:S(2)}, u32[]{:S(2)}) async-start(bf16[4,2,2,1,32,4096]{5,1,2,4,3,0:T(2,128)(2,1)} %copy.65), calls=%async_computation.4 | async-start | bytes 8388608 | tf_op jit(solution)/shard_map/all_to_all | solution.py:137
  363.4 10.8 %fusion.7 = bf16[4,32,4096]{2,0,1:T(4,128)(2,1)S(1)} fusion(bf16[2,2,4,32,4096]{4,0,1,3,2:T(2,128)(2,1)} %all-to-all-done.8, f32[4,2,1,4]{0,3,2,1:T(4,128)S(1)} %get-tuple-element.37, f32[4,2,1,4]{0,3,2,1:T(4,128)S(1)} %get-tuple-element.36), kind=kOutput, calls=%fused_computation.22 | convolution fusion | flops 101187712 | bytes 5243136 | tf_op jit(solution)/shard_map/lirgc,mlir->mgc/dot_general | solution.py:148
  374.2 1.6 copy.77
  375.7 34.5 %all-to-all-done.4 = bf16[4,2,2,1,32,4096]{5,1,2,4,3,0:T(2,128)(2,1)} async-done(((bf16[4,2,2,1,32,4096]{5,1,2,4,3,0:T(2,128)(2,1)}), bf16[4,2,2,1,32,4096]{5,1,2,4,3,0:T(2,128)(2,1)}, u32[]{:S(2)}, u32[]{:S(2)}) %all-to-all-start.4) | async-done | bytes 4194336 | tf_op jit(solution)/shard_map/all_to_all | solution.py:137
  410.2 3.5 all-to-all-start.9
  413.8 10.8 %fusion.6 = bf16[4,32,4096]{2,0,1:T(4,128)(2,1)S(1)} fusion(bf16[4,2,2,1,32,4096]{5,1,2,4,3,0:T(2,128)(2,1)} %all-to-all-done.4, f32[4,2,1,4]{0,3,2,1:T(4,128)S(1)} %get-tuple-element.37, f32[4,2,1,4]{0,3,2,1:T(4,128)S(1)} %get-tuple-element.36), kind=kOutput, calls=%fused_computation.21 | convolution fusion | flops 101187712 | bytes 5243136 | tf_op jit(solution)/shard_map/lirgc,mlir->mgc/dot_general | solution.py:148
  424.6 1.6 copy.68
  426.1 0.7 all-to-all-done.9
  426.9 3.7 all-to-all-start.5
  430.6 10.8 %fusion.8 = bf16[4,32,4096]{2,0,1:T(4,128)(2,1)S(1)} fusion(bf16[2,2,4,32,4096]{4,0,1,3,2:T(2,128)(2,1)} %all-to-all-done.10, f32[4,2,1,4]{0,3,2,1:T(4,128)S(1)} %get-tuple-element.37, f32[4,2,1,4]{0,3,2,1:T(4,128)S(1)} %get-tuple-element.36), kind=kOutput, calls=%fused_computation.23 | convolution fusion | flops 101187712 | bytes 5243136 | tf_op jit(solution)/shard_map/lirgc,mlir->mgc/dot_general | solution.py:148
  441.4 1.6 copy.83
  443.0 0.6 all-to-all-done.5
  443.6 3.6 all-to-all-start.11
  447.2 5.5 %fusion.15 = (bf16[1,128,4096]{2,1,0:T(8,128)(2,1)}, bf16[1,128,4096]{2,1,0:T(8,128)(2,1)}, bf16[1,128,4096]{2,1,0:T(8,128)(2,1)}) fusion(bf16[1,128,4096]{2,1,0:T(8,128)(2,1)} %param.8, bf16[1,128,4096]{2,1,0:T(8,128)(2,1)} %get-tuple-element.9, f32[4096]{0:T(1024)S(1)} %bitcast.157, bf16[1,128,4096]{2,1,0:T(8,128)(2,1)} %param.9, ...), kind=kLoop, calls=%fused_computation.45 | loop fusion | flops 8912896 | bytes 10502144 | tf_op jit(solution)/shard_map/convert_element_type | solution.py:167
  452.7 1.3 collective-permute-start
  454.0 6.2 %all-to-all-done.11 = bf16[4,32,4096]{2,1,0:T(8,128)(2,1)S(1)} async-done(((bf16[4,32,4096]{2,1,0:T(8,128)(2,1)}), bf16[4,32,4096]{2,1,0:T(8,128)(2,1)S(1)}, u32[]{:S(2)}, u32[]{:S(2)}) %all-to-all-start.11) | async-done | bytes 1048608 | tf_op jit(solution)/shard_map/all_to_all | solution.py:155
  460.2 0.7 multiply_reduce_fusion
  461.0 15.3 %all-reduce = (bf16[1,4096]{1,0:T(2,128)(2,1)S(1)}, bf16[1,4096]{1,0:T(2,128)(2,1)S(1)}) all-reduce(bf16[1,4096]{1,0:T(2,128)(2,1)S(1)} %broadcast_in_dim.10, bf16[1,4096]{1,0:T(2,128)(2,1)S(1)} %broadcast_in_dim.12), channel_id=1, replica_groups=mesh['section'=8,'ctx'=4] {'ctx'}, use_global_device_ids=true, to_apply=%region_1.2 | all-reduce | flops 8192 | bytes 32768 | tf_op jit(solution)/shard_map/psum | solution.py:173
  476.3 0.6 broadcast_in_dim.11
  476.9 0.6 broadcast_in_dim.13
  477.8 1.4 fusion.21
  479.1 1.0 copy.166
  (37 shorter events, 2.6 us)
Async XLA Ops:
  0.6 8.7 %copy-start.3 = (bf16[1,128,4096]{2,1,0:T(8,128)(2,1)S(1)}, bf16[1,128,4096]{2,1,0:T(8,128)(2,1)}, u32[]{:S(2)}) copy-start(bf16[1,128,4096]{2,1,0:T(8,128)(2,1)} %param.13) | copy-start | bytes 3145732
  0.6 8.7 %copy-start.2 = (bf16[1,128,4096]{2,1,0:T(8,128)(2,1)S(1)}, bf16[1,128,4096]{2,1,0:T(8,128)(2,1)}, u32[]{:S(2)}) copy-start(bf16[1,128,4096]{2,1,0:T(8,128)(2,1)} %param.8) | copy-start | bytes 3145732
  4.2 18.8 %all-to-all-start = ((bf16[4,32,4096]{2,1,0:T(8,128)(2,1)}), bf16[4,32,4096]{2,1,0:T(8,128)(2,1)S(1)}, u32[]{:S(2)}, u32[]{:S(2)}) async-start(bf16[4,32,4096]{2,1,0:T(8,128)(2,1)} %fusion.22), calls=%async_computation | async-start | bytes 2097152 | tf_op jit(solution)/shard_map/all_to_all | solution.py:100
  23.0 16.6 %all-to-all-start.6 = ((bf16[4,32,4096]{2,1,0:T(8,128)(2,1)}), bf16[4,32,4096]{2,1,0:T(8,128)(2,1)S(1)}, u32[]{:S(2)}, u32[]{:S(2)}) async-start(bf16[4,32,4096]{2,1,0:T(8,128)(2,1)} %bitcast.38), calls=%async_computation.6 | async-start | bytes 2097152 | tf_op jit(solution)/shard_map/all_to_all | solution.py:103
  39.6 16.6 %all-to-all-start.2 = ((bf16[4,32,4096]{2,1,0:T(8,128)(2,1)}), bf16[4,32,4096]{2,1,0:T(8,128)(2,1)S(1)}, u32[]{:S(2)}, u32[]{:S(2)}) async-start(bf16[4,32,4096]{2,1,0:T(8,128)(2,1)} %bitcast.17), calls=%async_computation.2 | async-start | bytes 2097152 | tf_op jit(solution)/shard_map/all_to_all | solution.py:97
  56.2 51.9 %all-to-all-start.7 = ((bf16[2,2,4,32,4096]{4,3,1,0,2:T(8,128)(2,1)}), bf16[2,2,4,32,4096]{4,3,1,0,2:T(8,128)(2,1)}, u32[]{:S(2)}, u32[]{:S(2)}) async-start(bf16[2,2,4,32,4096]{4,3,1,0,2:T(8,128)(2,1)} %copy.70), calls=%async_computation.7 | async-start | bytes 8388608 | tf_op jit(solution)/shard_map/all_to_all | solution.py:119
  108.0 52.0 %all-to-all-start.1 = ((bf16[2,2,4,32,4096]{4,3,1,0,2:T(8,128)(2,1)}), bf16[2,2,4,32,4096]{4,3,1,0,2:T(8,128)(2,1)}, u32[]{:S(2)}, u32[]{:S(2)}) async-start(bf16[2,2,4,32,4096]{4,3,1,0,2:T(8,128)(2,1)} %copy.54), calls=%async_computation.1 | async-start | bytes 8388608 | tf_op jit(solution)/shard_map/all_to_all | solution.py:116
  160.0 52.2 %all-to-all-start.3 = ((bf16[2,2,4,32,4096]{4,3,1,0,2:T(8,128)(2,1)}), bf16[2,2,4,32,4096]{4,3,1,0,2:T(8,128)(2,1)}, u32[]{:S(2)}, u32[]{:S(2)}) async-start(bf16[2,2,4,32,4096]{4,3,1,0,2:T(8,128)(2,1)} %copy.57), calls=%async_computation.3 | async-start | bytes 8388608 | tf_op jit(solution)/shard_map/all_to_all | solution.py:113
  212.2 8.3 %slice-start = ((s8[8388608]{0:T(1024)(128)(4,1)}), s8[4194304]{0:T(1024)(128)(4,1)S(1)}, s32[]{:S(2)}) async-start(s8[8388608]{0:T(1024)(128)(4,1)} %bitcast.134), calls=%async_computation.12 | async-start | bytes 8388608
  214.8 5.7 %slice-start.1 = ((s8[8388608]{0:T(1024)(128)(4,1)}), s8[4194304]{0:T(1024)(128)(4,1)S(1)}, s32[]{:S(2)}) async-start(s8[8388608]{0:T(1024)(128)(4,1)} %bitcast.134), calls=%async_computation.13 | async-start | bytes 8388608
  254.0 52.0 %all-to-all-start.10 = ((bf16[2,2,4,32,4096]{4,0,1,3,2:T(2,128)(2,1)}), bf16[2,2,4,32,4096]{4,0,1,3,2:T(2,128)(2,1)}, u32[]{:S(2)}, u32[]{:S(2)}) async-start(bf16[2,2,4,32,4096]{4,0,1,3,2:T(2,128)(2,1)} %copy.80), calls=%async_computation.10 | async-start | bytes 8388608 | tf_op jit(solution)/shard_map/all_to_all | solution.py:143
  306.0 52.0 %all-to-all-start.8 = ((bf16[2,2,4,32,4096]{4,0,1,3,2:T(2,128)(2,1)}), bf16[2,2,4,32,4096]{4,0,1,3,2:T(2,128)(2,1)}, u32[]{:S(2)}, u32[]{:S(2)}) async-start(bf16[2,2,4,32,4096]{4,0,1,3,2:T(2,128)(2,1)} %copy.74), calls=%async_computation.8 | async-start | bytes 8388608 | tf_op jit(solution)/shard_map/all_to_all | solution.py:142
  358.0 52.3 %all-to-all-start.4 = ((bf16[4,2,2,1,32,4096]{5,1,2,4,3,0:T(2,128)(2,1)}), bf16[4,2,2,1,32,4096]{5,1,2,4,3,0:T(2,128)(2,1)}, u32[]{:S(2)}, u32[]{:S(2)}) async-start(bf16[4,2,2,1,32,4096]{5,1,2,4,3,0:T(2,128)(2,1)} %copy.65), calls=%async_computation.4 | async-start | bytes 8388608 | tf_op jit(solution)/shard_map/all_to_all | solution.py:137
  410.2 16.6 %all-to-all-start.9 = ((bf16[4,32,4096]{2,1,0:T(8,128)(2,1)}), bf16[4,32,4096]{2,1,0:T(8,128)(2,1)S(1)}, u32[]{:S(2)}, u32[]{:S(2)}) async-start(bf16[4,32,4096]{2,1,0:T(8,128)(2,1)} %copy.77), calls=%async_computation.9 | async-start | bytes 2097152 | tf_op jit(solution)/shard_map/all_to_all | solution.py:154
  426.9 16.7 %all-to-all-start.5 = ((bf16[4,32,4096]{2,1,0:T(8,128)(2,1)}), bf16[4,32,4096]{2,1,0:T(8,128)(2,1)S(1)}, u32[]{:S(2)}, u32[]{:S(2)}) async-start(bf16[4,32,4096]{2,1,0:T(8,128)(2,1)} %copy.68), calls=%async_computation.5 | async-start | bytes 2097152 | tf_op jit(solution)/shard_map/all_to_all | solution.py:153
  441.4 5.7 %copy-start.4 = (f32[1,4096]{1,0:T(1,128)S(1)}, f32[1,4096]{1,0:T(1,128)}, u32[]{:S(2)}) copy-start(f32[1,4096]{1,0:T(1,128)} %param.12) | copy-start | bytes 49156
  443.6 3.6 copy-start.1
  443.6 16.6 %all-to-all-start.11 = ((bf16[4,32,4096]{2,1,0:T(8,128)(2,1)}), bf16[4,32,4096]{2,1,0:T(8,128)(2,1)S(1)}, u32[]{:S(2)}, u32[]{:S(2)}) async-start(bf16[4,32,4096]{2,1,0:T(8,128)(2,1)} %copy.83), calls=%async_computation.11 | async-start | bytes 2097152 | tf_op jit(solution)/shard_map/all_to_all | solution.py:155
  447.2 13.0 %copy-start = (bf16[1,128,4096]{2,1,0:T(8,128)(2,1)S(1)}, bf16[1,128,4096]{2,1,0:T(8,128)(2,1)}, u32[]{:S(2)}) copy-start(bf16[1,128,4096]{2,1,0:T(8,128)(2,1)} %param.10) | copy-start | bytes 3145732
  452.7 26.4 %collective-permute-start = (bf16[1,128,4096]{2,1,0:T(8,128)(2,1)}, bf16[1,128,4096]{2,1,0:T(8,128)(2,1)S(1)}, u32[]{:S(2)}, u32[]{:S(2)}) collective-permute-start(bf16[1,128,4096]{2,1,0:T(8,128)(2,1)} %get-tuple-element.23), channel_id=1, source_target_pairs={{4,0},{8,4},{12,8},{16,12},{20,16},{24,20},{28,24},{5,1},{9,5},{13... | collective-permute-start | bytes 3145736 | tf_op jit(solution)/shard_map/ppermute | solution.py:13
